TPU v7x, 32 devices: a whole 2x2x4 slice. The times are simulated.
32 devices in a mesh: island: 4 (over y, x), shard: 8 (over z, core).
Axes of the slice: x: 2, y: 2, z: 4, core: 2. Of those that a mesh axis runs over, the one named last changes fastest.
Arguments:
- gate_pre: bfloat16 [16384, 256], P(('island', 'shard')), may hold values from -6 to 6
- up_pre: bfloat16 [16384, 256], P(('island', 'shard')), may hold values from -6 to 6
- grad_out: bfloat16 [16384, 8192], P(('island', 'shard')), may hold values from -6 to 6
- token_ids: int32 [16384], P(('island', 'shard')), may hold values from 0 to 128255, as said below
- step_count: int32 [1], replicated, may hold values from 0 to 999
- island_drift: float32 [4, 256, 8192], P('island', 'shard'), may hold values from -4 to 4
- adam_m: float32 [4, 256, 8192], P('island', 'shard'), may hold values from -0.015625 to 0.015625
- adam_v: float32 [4, 256, 8192], P('island', 'shard'), may hold values from 3.8146972e-08 to 6.1035155e-07
- anchor: float32 [256, 8192], P('shard'), may hold values from -6 to 6
- momentum: float32 [256, 8192], P('shard'), may hold values from -4 to 4
- next_hidden: bfloat16 [16384, 256], P(('island', 'shard')), may hold values from -6 to 6
Outputs:
- new_anchor: float32 [256, 8192], P('shard', 'island')
- new_momentum: float32 [256, 8192], P('shard', 'island')
- next_out: bfloat16 [16384, 8192], P(('island', 'shard'))
- live_share: float32 [4], P('island')
Inputs may be any that keep to these rules, and one draw needn't show every extreme that they name: `token_ids`: 0 marks padding; within each aligned block of 512 rows the padding comes last, and a third or more of the block's rows are tokens.
All inputs are finite; a program needn't handle non-finite values.
Results may differ from a plain program's by a relative error of at most 0.0004.
The roundings to bfloat16 on the way count: a program that leaves them out, or rounds other values in their place, can miss the bound.
Values may be sent and summed in bfloat16 or wider, within the bound.
A program may use at most 128 MiB of HBM per device.

v0:
```python
import math
import jax
import jax.numpy as jnp
from jax import lax
from jax.sharding import PartitionSpec as P

peak_rate = 0.25
beta_one = 0.9
beta_two = 0.95
adam_eps = 1e-08
decay_rate = 0.1
outer_rate = 0.7
outer_beta = 0.9


def shards(
    gate_pre,
    up_pre,
    grad_out,
    token_ids,
    step_count,
    island_drift,
    adam_m,
    adam_v,
    anchor,
    momentum,
    next_hidden,
):
    row_count = anchor.shape[0]
    width = anchor.shape[1]
    islands = lax.axis_size("island")
    factor = float(row_count * lax.axis_size("shard")) ** (-0.5)
    hidden = (jax.nn.silu(gate_pre.astype(jnp.float32)) * up_pre.astype(jnp.float32)).astype(
        jnp.bfloat16
    )
    live_rows = token_ids != 0
    masked = jnp.where(live_rows[:, None], grad_out, jnp.zeros_like(grad_out))
    tally = lax.psum(jnp.sum(live_rows.astype(jnp.float32)), "shard")
    slot_total = float(token_ids.shape[0] * lax.axis_size("shard"))
    live_share = jnp.reshape(tally / slot_total, (1,))
    columns = hidden
    reduced = lax.psum_scatter(
        lax.dot_general(
            columns, masked, (((0,), (0,)), ((), ())), preferred_element_type=jnp.float32
        )
        * factor,
        "shard",
        scatter_dimension=0,
        tiled=True,
    )
    gradient = reduced / tally
    moment = step_count[0].astype(jnp.float32)
    inner_rate = (
        peak_rate
        * jnp.minimum(1.0, (moment + 1.0) / 100.0)
        * (0.1 + 0.45 * (1.0 + jnp.cos(math.pi * moment / 1000.0)))
    )
    bias_one = 1.0 - jnp.power(jnp.float32(beta_one), moment + 1.0)
    bias_two = 1.0 - jnp.power(jnp.float32(beta_two), moment + 1.0)
    first_moment = beta_one * adam_m[0] + (1.0 - beta_one) * gradient
    second_moment = beta_two * adam_v[0] + (1.0 - beta_two) * gradient * gradient
    direction = first_moment / bias_one / (jnp.sqrt(second_moment / bias_two) + adam_eps)
    params = anchor + island_drift[0]
    updated = params - inner_rate * (direction + decay_rate * params)
    change = anchor - updated
    col_count = width // islands
    col_start = lax.axis_index("island") * col_count
    mean_change = lax.psum(change, "island") / islands
    full_momentum = outer_beta * momentum + mean_change
    full_anchor = anchor - outer_rate * (mean_change + outer_beta * full_momentum)
    weights = full_anchor.astype(jnp.bfloat16)
    new_anchor = lax.dynamic_slice_in_dim(full_anchor, col_start, col_count, 1)
    new_momentum = lax.dynamic_slice_in_dim(full_momentum, col_start, col_count, 1)
    columns = next_hidden
    produced = jnp.dot(
        columns,
        lax.all_gather(weights, "shard", axis=0, tiled=True),
        preferred_element_type=jnp.float32,
    )
    next_out = (produced * factor).astype(jnp.bfloat16)
    return (new_anchor, new_momentum, next_out, live_share)


def solution(mesh):
    in_specs = (
        P(("island", "shard"), None),
        P(("island", "shard"), None),
        P(("island", "shard"), None),
        P(("island", "shard")),
        P(),
        P("island", "shard", None),
        P("island", "shard", None),
        P("island", "shard", None),
        P("shard", None),
        P("shard", None),
        P(("island", "shard"), None),
    )
    out_specs = (
        P("shard", "island"),
        P("shard", "island"),
        P(("island", "shard"), None),
        P("island"),
    )
    return jax.shard_map(shards, mesh=mesh, in_specs=in_specs, out_specs=out_specs, check_vma=False)
```

profile of v0, /device:TPU:0, one launch (start us, length us, event | category | flops | bytes accessed | tf_op | source)
XLA Modules:
  0.0 242.8 jit_solution(4508063332395682022)
XLA Ops:
  7.2 0.0 copy-start
  7.2 0.0 reduce-scatter.2.cloned.1.call-start
  7.2 1.3 convert_reduce_fusion
  8.5 9.5 %convolution_multiply_fusion = f32[256,8192]{1,0:T(8,128)} fusion(bf16[512,8192]{1,0:T(8,128)(2,1)} %param.13, pred[512]{0:T(512)(128)(4,1)S(1)} %get-tuple-element.11, bf16[512,256]{1,0:T(8,128)(2,1)} %param.12, bf16[512,256]{1,0:T(8,128)(2,1)} %param.11), kind=kOutput, calls=%fused_computation.2 | convolution fusion | flops 2154823680 | bytes 17302016 | tf_op jit(solution)/shard_map/dot_general | solution.py:43
  18.0 0.0 copy-start.1
  18.0 0.0 copy-start.2
  18.0 0.0 copy-start.3
  18.0 0.0 reduce-scatter.2.cloned.1.call-update
  18.1 0.0 all-reduce.2.cloned.1.call-start
  18.1 19.4 %psum.14 = f32[]{:T(128)} all-reduce(f32[]{:T(128)} %get-tuple-element.10), channel_id=1, replica_groups=mesh['island'=4,'shard'=8] {'shard'}, use_global_device_ids=true, to_apply=%region_2.3 | all-reduce | flops 1 | bytes 8 | tf_op jit(solution)/shard_map/psum | solution.py:38
  38.3 72.3 %reduce-scatter.2.cloned.1.call-done = f32[32,8192]{1,0:T(8,128)} async-done(((f32[256,8192]{1,0:T(8,128)}), f32[32,8192]{1,0:T(8,128)}) %reduce-scatter.2.cloned.1.call-update) | async-done | bytes 1048592 | tf_op jit(solution)/shard_map/reduce_scatter | solution.py:42
  110.6 0.0 copy-done.1
  110.6 0.0 copy-done.2
  110.6 0.0 copy-done.3
  110.6 4.1 %subtract_subtract_fusion = f32[32,8192]{1,0:T(8,128)} fusion(f32[32,8192]{1,0:T(8,128)S(1)} %copy-done.1, f32[1,32,8192]{2,1,0:T(8,128)S(1)} %copy-done.2, f32[1,32,8192]{2,1,0:T(8,128)S(1)} %copy-done.3, f32[32,8192]{1,0:T(8,128)} %reduce-scatter.2.cloned.1.call-done, f32[1,32,8192]{2,1,0:T(8,128)} %param.17, f32[]{:T(128)} %bitcast.5, f32[]{:T(128)} %bitcast.3, ...), kind=kLoop, calls=%fused_computation.17 | loop fusion | flops 4718592 | bytes 6291472 | tf_op jit(solution)/shard_map/sub | solution.py:65
  114.6 0.0 all-reduce.2.cloned.1.call-update
  114.7 0.0 all-gather.2.cloned.1.call-start
  114.7 51.1 %all-reduce.2.cloned.1.call-done = f32[32,8192]{1,0:T(8,128)} async-done(((f32[32,8192]{1,0:T(8,128)}), f32[32,8192]{1,0:T(8,128)}) %all-reduce.2.cloned.1.call-update) | async-done | bytes 1048592 | tf_op jit(solution)/shard_map/psum | solution.py:68
  165.8 2.6 %fusion.19 = (bf16[32,8192]{1,0:T(8,128)(2,1)}, f32[32,8192]{1,0:T(8,128)S(1)}, f32[32,8192]{1,0:T(8,128)S(1)}) fusion(f32[32,8192]{1,0:T(8,128)S(1)} %copy-done.1, f32[32,8192]{1,0:T(8,128)} %param.20, f32[32,8192]{1,0:T(8,128)} %all-reduce.2.cloned.1.call-done), kind=kLoop, calls=%fused_computation.32 | loop fusion | flops 2097152 | bytes 5767168 | tf_op jit(solution)/shard_map/convert_element_type | solution.py:71
  168.4 0.0 all-gather.2.cloned.1.call-update
  169.1 0.8 constant_dynamic-slice_fusion
  169.9 45.5 %all-gather.2.cloned.1.call-done = bf16[256,8192]{1,0:T(8,128)(2,1)} async-done(((bf16[32,8192]{1,0:T(8,128)(2,1)}), bf16[256,8192]{1,0:T(8,128)(2,1)}) %all-gather.2.cloned.1.call-update) | async-done | bytes 4194320 | tf_op jit(solution)/shard_map/all_gather | solution.py:77
  215.5 0.0 copy-done
  215.5 7.8 %fusion = bf16[512,8192]{0,1:T(8,128)(2,1)} fusion(bf16[256,8192]{1,0:T(8,128)(2,1)} %all-gather.2.cloned.1.call-done, bf16[512,256]{1,0:T(8,128)(2,1)S(1)} %copy-done), kind=kOutput, calls=%fused_computation.1 | convolution fusion | flops 2155872256 | bytes 12845056 | tf_op jit(solution)/shard_map/dot_general | solution.py:75
  223.3 11.9 %copy.15 = bf16[512,8192]{1,0:T(8,128)(2,1)} copy(bf16[512,8192]{0,1:T(8,128)(2,1)} %fusion) | data formatting | bytes 16777216
Async XLA Ops:
  7.2 208.3 %copy-start = (bf16[512,256]{1,0:T(8,128)(2,1)S(1)}, bf16[512,256]{1,0:T(8,128)(2,1)}, u32[]{:S(2)}) copy-start(bf16[512,256]{1,0:T(8,128)(2,1)} %param.21) | copy-start | bytes 786436
  7.2 103.4 %reduce-scatter.2.cloned.1.call-start = ((), (), s32[]{:S(2)}) async-start(), calls=%async_computation.1 | async-start | bytes 9437184 | tf_op jit(solution)/shard_map/reduce_scatter | solution.py:42
  18.0 92.6 %copy-start.1 = (f32[32,8192]{1,0:T(8,128)S(1)}, f32[32,8192]{1,0:T(8,128)}, u32[]{:S(2)}) copy-start(f32[32,8192]{1,0:T(8,128)} %param.19) | copy-start | bytes 3145732
  18.0 92.6 %copy-start.2 = (f32[1,32,8192]{2,1,0:T(8,128)S(1)}, f32[1,32,8192]{2,1,0:T(8,128)}, u32[]{:S(2)}) copy-start(f32[1,32,8192]{2,1,0:T(8,128)} %param.16) | copy-start | bytes 3145732
  18.0 92.6 %copy-start.3 = (f32[1,32,8192]{2,1,0:T(8,128)S(1)}, f32[1,32,8192]{2,1,0:T(8,128)}, u32[]{:S(2)}) copy-start(f32[1,32,8192]{2,1,0:T(8,128)} %param.18) | copy-start | bytes 3145732
  18.1 147.7 %all-reduce.2.cloned.1.call-start = ((), (), s32[]{:S(2)}) async-start(), calls=%async_computation.2 | async-start | bytes 2097152 | tf_op jit(solution)/shard_map/psum | solution.py:68
  114.7 100.8 %all-gather.2.cloned.1.call-start = ((), (), s32[]{:S(2)}) async-start(), calls=%async_computation.3 | async-start | bytes 4718592 | tf_op jit(solution)/shard_map/all_gather | solution.py:77
Sparse Core Ops, SparseCore 0:
  18.2 92.3 reduce-scatter.1
  114.8 50.9 all-reduce.1
  168.6 46.8 all-gather.1
where the time goes:
time: 243 us
  waiting for transfers between devices  169 us (70%)
  blocking collectives  19.4 us (8%)
  matrix products  17.3 us (7%)
  between operations  16.4 us (7%)
  local copies, waits for them, and re-layouts  12.8 us (5%)
  other arithmetic  8 us (3%)
    reduce_scatter x1, waiting for transfers between devices, shards(): lax.psum_scatter(lax.dot_general(columns, masked, (((0,), (0,)), ((), ())...  72.3 us
    psum x1, waiting for transfers between devices, shards(): mean_change = lax.psum(change, 'island') / islands  51.1 us
    all_gather x1, waiting for transfers between devices, shards(): lax.all_gather(weights, 'shard', axis=0, tiled=True)  45.5 us
    psum x1, blocking collectives, shards(): tally = lax.psum(jnp.sum(live_rows.astype(jnp.float32)), 'shard')  19.4 us
    unnamed x9, local copies, waits for them, and re-layouts  11.9 us
    dot_general x1, matrix products, shards(): lax.dot_general(columns, masked, (((0,), (0,)), ((), ())), preferred_elem...  9.47 us
    dot_general x1, matrix products, shards(): jnp.dot(columns, lax.all_gather(weights, 'shard', axis=0, tiled=True), pr...  7.81 us
  transfers between devices with their start and end apart: 3, of which 3 were waited for; matrix products, arithmetic and copies ran while one was open for 0% of the time, Pallas kernels for 0%

commit v1 on v0

--- a/solution.py
+++ b/solution.py
@@ -11,6 +11,22 @@
 decay_rate = 0.1
 outer_rate = 0.7
 outer_beta = 0.9
+
+
+def collect(x, axis, dim):
+    ways, here, step = (lax.axis_size(axis), lax.axis_index(axis), x.shape[dim])
+    shape = [n * ways if d == dim else n for d, n in enumerate(x.shape)]
+    full = lax.dynamic_update_slice_in_dim(jnp.zeros(shape, x.dtype), x, here * step, axis=dim)
+    going_up = going_down = x
+    for far in range(1, ways // 2 + 1):
+        going_up = lax.ppermute(going_up, axis, [(d, (d + 1) % ways) for d in range(ways)])
+        full = lax.dynamic_update_slice_in_dim(full, going_up, (here - far) % ways * step, axis=dim)
+        if 2 * far < ways:
+            going_down = lax.ppermute(going_down, axis, [(d, (d - 1) % ways) for d in range(ways)])
+            full = lax.dynamic_update_slice_in_dim(
+                full, going_down, (here + far) % ways * step, axis=dim
+            )
+    return full
 
 
 def shards(
@@ -72,11 +88,7 @@
     new_anchor = lax.dynamic_slice_in_dim(full_anchor, col_start, col_count, 1)
     new_momentum = lax.dynamic_slice_in_dim(full_momentum, col_start, col_count, 1)
     columns = next_hidden
-    produced = jnp.dot(
-        columns,
-        lax.all_gather(weights, "shard", axis=0, tiled=True),
-        preferred_element_type=jnp.float32,
-    )
+    produced = jnp.dot(columns, collect(weights, "shard", 0), preferred_element_type=jnp.float32)
     next_out = (produced * factor).astype(jnp.bfloat16)
     return (new_anchor, new_momentum, next_out, live_share)
 

time: 243 us -> 249 us (1.025)
  starting transfers between devices: 0.12 us -> 10.8 us
  waiting for transfers between devices: 169 us -> 165 us
    all_gather x1 -> x0, waiting for transfers between devices: 45.5 us -> none  [shards(): lax.all_gather(weights, 'shard', axis=0, tiled=True)]
    ppermute x0 -> x7, waiting for transfers between devices: none -> 42.7 us  [the longest x4 42.7 us: collect(): lax.ppermute(going_up, axis, [(d, (d + 1) % ways) for d in range(ways)])]
    ppermute x0 -> x7, starting transfers between devices: none -> 10.7 us  [the longest x3 10.6 us: collect(): lax.ppermute(going_down, axis, [(d, (d - 1) % ways) for d in range(ways)])]
    convert_element_type x1 -> x0, other arithmetic: 2.62 us -> none  [shards(): weights = full_anchor.astype(jnp.bfloat16)]
    unnamed x9 -> x13, local copies, waits for them, and re-layouts: 11.9 us -> 12.7 us
  transfers between devices with their start and end apart: 3 -> 9, of which waited for: 3 -> 6; matrix products, arithmetic and copies ran while one was open for 0% -> 1% of each run, Pallas kernels for 0% -> 0%
where the time goes in v1:
time: 249 us; the launch traced here: 248 us
  waiting for transfers between devices  165 us (66%)
  blocking collectives  19.4 us (8%)
  between operations  17 us (7%)
  matrix products  15.1 us (6%)
  local copies, waits for them, and re-layouts  14.9 us (6%)
  starting transfers between devices  10.8 us (4%)
  other arithmetic  5.8 us (2%)
    reduce_scatter x1, waiting for transfers between devices, shards(): lax.psum_scatter(lax.dot_general(columns, masked, (((0,), (0,)), ((), ())...  72.3 us
    psum x1, waiting for transfers between devices, shards(): mean_change = lax.psum(change, 'island') / islands  50.3 us
    ppermute x4, waiting for transfers between devices, collect(): lax.ppermute(going_up, axis, [(d, (d + 1) % ways) for d in range(ways)])  42.7 us
    psum x1, blocking collectives, shards(): tally = lax.psum(jnp.sum(live_rows.astype(jnp.float32)), 'shard')  19.4 us
    unnamed x13, local copies, waits for them, and re-layouts  12.7 us
    ppermute x3, starting transfers between devices, collect(): lax.ppermute(going_down, axis, [(d, (d - 1) % ways) for d in range(ways)])  10.6 us
    dot_general x1, matrix products, shards(): lax.dot_general(columns, masked, (((0,), (0,)), ((), ())), preferred_elem...  9.47 us
    dot_general x1, matrix products, shards(): jnp.dot(columns, collect(weights, 'shard', 0), preferred_element_type=jnp...  5.64 us
  transfers between devices with their start and end apart: 9, of which 6 were waited for; matrix products, arithmetic and copies ran while one was open for 1% of the time, Pallas kernels for 0%

profile of v1, /device:TPU:0, one launch (start us, length us, event | category | flops | bytes accessed | tf_op | source)
XLA Modules:
  0.0 248.2 jit_solution(5141368212673598155)
XLA Ops:
  7.2 0.0 copy-start
  7.2 0.0 reduce-scatter.2.cloned.1.call-start
  7.2 1.3 convert_reduce_fusion
  8.5 9.5 %convolution_multiply_fusion = f32[256,8192]{1,0:T(8,128)} fusion(bf16[512,8192]{1,0:T(8,128)(2,1)} %param.13, pred[512]{0:T(512)(128)(4,1)S(1)} %get-tuple-element.12, bf16[512,256]{1,0:T(8,128)(2,1)} %param.12, bf16[512,256]{1,0:T(8,128)(2,1)} %param.11), kind=kOutput, calls=%fused_computation.2 | convolution fusion | flops 2154823680 | bytes 17302016 | tf_op jit(solution)/shard_map/dot_general | solution.py:59
  18.0 0.0 reduce-scatter.2.cloned.1.call-update
  18.1 0.0 all-reduce.2.cloned.1.call-start
  18.1 19.4 %psum.14 = f32[]{:T(128)} all-reduce(f32[]{:T(128)} %get-tuple-element.11), channel_id=1, replica_groups=mesh['island'=4,'shard'=8] {'shard'}, use_global_device_ids=true, to_apply=%region_2.3 | all-reduce | flops 1 | bytes 8 | tf_op jit(solution)/shard_map/psum | solution.py:54
  38.3 72.3 %reduce-scatter.2.cloned.1.call-done = f32[32,8192]{1,0:T(8,128)} async-done(((f32[256,8192]{1,0:T(8,128)}), f32[32,8192]{1,0:T(8,128)}) %reduce-scatter.2.cloned.1.call-update) | async-done | bytes 1048592 | tf_op jit(solution)/shard_map/reduce_scatter | solution.py:58
  110.6 4.1 %subtract_subtract_fusion = f32[32,8192]{1,0:T(8,128)} fusion(f32[32,8192]{1,0:T(8,128)S(1)} %copy-done.3, f32[1,32,8192]{2,1,0:T(8,128)S(1)} %copy-done.4, f32[1,32,8192]{2,1,0:T(8,128)S(1)} %copy-done.5, f32[32,8192]{1,0:T(8,128)} %reduce-scatter.2.cloned.1.call-done, f32[1,32,8192]{2,1,0:T(8,128)} %param.17, f32[]{:T(128)} %bitcast.5, f32[]{:T(128)} %bitcast.3, ...), kind=kLoop, calls=%fused_computation.17 | loop fusion | flops 4718592 | bytes 6291472 | tf_op jit(solution)/shard_map/sub | solution.py:81
  114.6 0.0 all-reduce.2.cloned.1.call-update
  115.5 50.3 %all-reduce.2.cloned.1.call-done = f32[32,8192]{1,0:T(8,128)} async-done(((f32[32,8192]{1,0:T(8,128)}), f32[32,8192]{1,0:T(8,128)}) %all-reduce.2.cloned.1.call-update) | async-done | bytes 1048592 | tf_op jit(solution)/shard_map/psum | solution.py:84
  165.8 0.5 broadcast_in_dim.17
  166.3 0.7 copy-done.2
  167.0 0.3 constant_dynamic-update-slice_fusion.7
  167.3 0.1 collective-permute-start
  167.4 3.5 %collective-permute-start.1 = (bf16[32,8192]{1,0:T(8,128)(2,1)S(1)}, bf16[32,8192]{1,0:T(8,128)(2,1)S(1)}, u32[]{:S(2)}, u32[]{:S(2)}) collective-permute-start(bf16[32,8192]{1,0:T(8,128)(2,1)S(1)} %get-tuple-element.9), channel_id=1, source_target_pairs={{0,7},{1,0},{2,1},{3,2},{4,3},{5,4},{6,5},{7,6},{8,15},{9,8},{10,9... | collective-permute-start | bytes 1572872 | tf_op jit(solution)/shard_map/ppermute | solution.py:25
  170.9 0.1 multiply_add_fusion
  171.0 0.7 constant_dynamic-slice_fusion
  171.8 0.7 constant_dynamic-slice_fusion.1
  172.5 9.1 %collective-permute-done = bf16[32,8192]{1,0:T(8,128)(2,1)S(1)} collective-permute-done((bf16[32,8192]{1,0:T(8,128)(2,1)S(1)}, bf16[32,8192]{1,0:T(8,128)(2,1)S(1)}, u32[]{:S(2)}, u32[]{:S(2)}) %collective-permute-start) | collective-permute-done | bytes 524320 | tf_op jit(solution)/shard_map/ppermute | solution.py:22
  181.6 0.0 collective-permute-start.2
  181.6 0.0 collective-permute-done.1
  181.6 3.5 %collective-permute-start.3 = (bf16[32,8192]{1,0:T(8,128)(2,1)S(1)}, bf16[32,8192]{1,0:T(8,128)(2,1)S(1)}, u32[]{:S(2)}, u32[]{:S(2)}) collective-permute-start(bf16[32,8192]{1,0:T(8,128)(2,1)S(1)} %collective-permute-done.1), channel_id=1, source_target_pairs={{0,7},{1,0},{2,1},{3,2},{4,3},{5,4},{6,5},{7,6},{8,15},{9,8},{10,9... | collective-permute-start | bytes 1572872 | tf_op jit(solution)/shard_map/ppermute | solution.py:25
  185.2 12.4 %collective-permute-done.2 = bf16[32,8192]{1,0:T(8,128)(2,1)S(1)} collective-permute-done((bf16[32,8192]{1,0:T(8,128)(2,1)S(1)}, bf16[32,8192]{1,0:T(8,128)(2,1)S(1)}, u32[]{:S(2)}, u32[]{:S(2)}) %collective-permute-start.2) | collective-permute-done | bytes 524320 | tf_op jit(solution)/shard_map/ppermute | solution.py:22
  197.6 0.0 collective-permute-start.4
  197.6 0.0 collective-permute-done.3
  197.6 3.5 %collective-permute-start.5 = (bf16[32,8192]{1,0:T(8,128)(2,1)S(1)}, bf16[32,8192]{1,0:T(8,128)(2,1)S(1)}, u32[]{:S(2)}, u32[]{:S(2)}) collective-permute-start(bf16[32,8192]{1,0:T(8,128)(2,1)S(1)} %collective-permute-done.3), channel_id=1, source_target_pairs={{0,7},{1,0},{2,1},{3,2},{4,3},{5,4},{6,5},{7,6},{8,15},{9,8},{10,9... | collective-permute-start | bytes 1572872 | tf_op jit(solution)/shard_map/ppermute | solution.py:25
  201.2 11.0 %collective-permute-done.4 = bf16[32,8192]{1,0:T(8,128)(2,1)S(1)} collective-permute-done((bf16[32,8192]{1,0:T(8,128)(2,1)S(1)}, bf16[32,8192]{1,0:T(8,128)(2,1)S(1)}, u32[]{:S(2)}, u32[]{:S(2)}) %collective-permute-start.4) | collective-permute-done | bytes 524320 | tf_op jit(solution)/shard_map/ppermute | solution.py:22
  212.2 0.0 collective-permute-start.6
  212.3 10.3 %collective-permute-done.6 = bf16[32,8192]{1,0:T(8,128)(2,1)S(1)} collective-permute-done((bf16[32,8192]{1,0:T(8,128)(2,1)S(1)}, bf16[32,8192]{1,0:T(8,128)(2,1)S(1)}, u32[]{:S(2)}, u32[]{:S(2)}) %collective-permute-start.6) | collective-permute-done | bytes 524320 | tf_op jit(solution)/shard_map/ppermute | solution.py:22
  222.7 5.6 %fusion = bf16[512,8192]{0,1:T(8,128)(2,1)} fusion(bf16[256,8192]{1,0:T(8,128)(2,1)S(1)} %constant_dynamic-update-slice_fusion, bf16[512,256]{1,0:T(8,128)(2,1)S(1)} %copy-done), kind=kOutput, calls=%fused_computation.1 | convolution fusion | flops 2155872256 | bytes 12845056 | tf_op jit(solution)/shard_map/dot_general | solution.py:91
  228.3 11.9 %copy.15 = bf16[512,8192]{1,0:T(8,128)(2,1)} copy(bf16[512,8192]{0,1:T(8,128)(2,1)} %fusion) | data formatting | bytes 16777216
  (18 shorter events, 0.3 us)
Async XLA Ops:
  7.2 215.5 %copy-start = (bf16[512,256]{1,0:T(8,128)(2,1)S(1)}, bf16[512,256]{1,0:T(8,128)(2,1)}, u32[]{:S(2)}) copy-start(bf16[512,256]{1,0:T(8,128)(2,1)} %param.21) | copy-start | bytes 786436
  7.2 103.4 %reduce-scatter.2.cloned.1.call-start = ((), (), s32[]{:S(2)}) async-start(), calls=%async_computation.1 | async-start | bytes 9437184 | tf_op jit(solution)/shard_map/reduce_scatter | solution.py:58
  18.0 92.6 %copy-start.3 = (f32[32,8192]{1,0:T(8,128)S(1)}, f32[32,8192]{1,0:T(8,128)}, u32[]{:S(2)}) copy-start(f32[32,8192]{1,0:T(8,128)} %param.19) | copy-start | bytes 3145732
  18.0 92.6 %copy-start.4 = (f32[1,32,8192]{2,1,0:T(8,128)S(1)}, f32[1,32,8192]{2,1,0:T(8,128)}, u32[]{:S(2)}) copy-start(f32[1,32,8192]{2,1,0:T(8,128)} %param.16) | copy-start | bytes 3145732
  18.0 92.6 %copy-start.5 = (f32[1,32,8192]{2,1,0:T(8,128)S(1)}, f32[1,32,8192]{2,1,0:T(8,128)}, u32[]{:S(2)}) copy-start(f32[1,32,8192]{2,1,0:T(8,128)} %param.18) | copy-start | bytes 3145732
  18.1 147.7 %all-reduce.2.cloned.1.call-start = ((), (), s32[]{:S(2)}) async-start(), calls=%async_computation.2 | async-start | bytes 2097152 | tf_op jit(solution)/shard_map/psum | solution.py:84
  114.6 51.6 %copy-start.1 = (f32[32,8192]{1,0:T(8,128)S(1)}, f32[32,8192]{1,0:T(8,128)}, u32[]{:S(2)}) copy-start(f32[32,8192]{1,0:T(8,128)} %param.20) | copy-start | bytes 3145732
  165.8 1.2 copy-start.2
  167.3 14.3 %collective-permute-start = (bf16[32,8192]{1,0:T(8,128)(2,1)S(1)}, bf16[32,8192]{1,0:T(8,128)(2,1)S(1)}, u32[]{:S(2)}, u32[]{:S(2)}) collective-permute-start(bf16[32,8192]{1,0:T(8,128)(2,1)S(1)} %get-tuple-element.9), channel_id=1, source_target_pairs={{0,1},{1,2},{2,3},{3,4},{4,5},{5,6},{6,7},{7,0},{8,9},{9,10},{10,1... | collective-permute-start | bytes 1572872 | tf_op jit(solution)/shard_map/ppermute | solution.py:22
  167.4 14.2 %collective-permute-start.1 = (bf16[32,8192]{1,0:T(8,128)(2,1)S(1)}, bf16[32,8192]{1,0:T(8,128)(2,1)S(1)}, u32[]{:S(2)}, u32[]{:S(2)}) collective-permute-start(bf16[32,8192]{1,0:T(8,128)(2,1)S(1)} %get-tuple-element.9), channel_id=1, source_target_pairs={{0,7},{1,0},{2,1},{3,2},{4,3},{5,4},{6,5},{7,6},{8,15},{9,8},{10,9... | collective-permute-start | bytes 1572872 | tf_op jit(solution)/shard_map/ppermute | solution.py:25
  181.6 16.0 %collective-permute-start.2 = (bf16[32,8192]{1,0:T(8,128)(2,1)S(1)}, bf16[32,8192]{1,0:T(8,128)(2,1)S(1)}, u32[]{:S(2)}, u32[]{:S(2)}) collective-permute-start(bf16[32,8192]{1,0:T(8,128)(2,1)S(1)} %collective-permute-done), channel_id=1, source_target_pairs={{0,1},{1,2},{2,3},{3,4},{4,5},{5,6},{6,7},{7,0},{8,9},{9,10},{10,1... | collective-permute-start | bytes 1572872 | tf_op jit(solution)/shard_map/ppermute | solution.py:22
  181.6 16.0 %collective-permute-start.3 = (bf16[32,8192]{1,0:T(8,128)(2,1)S(1)}, bf16[32,8192]{1,0:T(8,128)(2,1)S(1)}, u32[]{:S(2)}, u32[]{:S(2)}) collective-permute-start(bf16[32,8192]{1,0:T(8,128)(2,1)S(1)} %collective-permute-done.1), channel_id=1, source_target_pairs={{0,7},{1,0},{2,1},{3,2},{4,3},{5,4},{6,5},{7,6},{8,15},{9,8},{10,9... | collective-permute-start | bytes 1572872 | tf_op jit(solution)/shard_map/ppermute | solution.py:25
  197.6 14.7 %collective-permute-start.4 = (bf16[32,8192]{1,0:T(8,128)(2,1)S(1)}, bf16[32,8192]{1,0:T(8,128)(2,1)S(1)}, u32[]{:S(2)}, u32[]{:S(2)}) collective-permute-start(bf16[32,8192]{1,0:T(8,128)(2,1)S(1)} %collective-permute-done.2), channel_id=1, source_target_pairs={{0,1},{1,2},{2,3},{3,4},{4,5},{5,6},{6,7},{7,0},{8,9},{9,10},{10,1... | collective-permute-start | bytes 1572872 | tf_op jit(solution)/shard_map/ppermute | solution.py:22
  197.6 14.7 %collective-permute-start.5 = (bf16[32,8192]{1,0:T(8,128)(2,1)S(1)}, bf16[32,8192]{1,0:T(8,128)(2,1)S(1)}, u32[]{:S(2)}, u32[]{:S(2)}) collective-permute-start(bf16[32,8192]{1,0:T(8,128)(2,1)S(1)} %collective-permute-done.3), channel_id=1, source_target_pairs={{0,7},{1,0},{2,1},{3,2},{4,3},{5,4},{6,5},{7,6},{8,15},{9,8},{10,9... | collective-permute-start | bytes 1572872 | tf_op jit(solution)/shard_map/ppermute | solution.py:25
  212.2 10.4 %collective-permute-start.6 = (bf16[32,8192]{1,0:T(8,128)(2,1)S(1)}, bf16[32,8192]{1,0:T(8,128)(2,1)S(1)}, u32[]{:S(2)}, u32[]{:S(2)}) collective-permute-start(bf16[32,8192]{1,0:T(8,128)(2,1)S(1)} %collective-permute-done.4), channel_id=1, source_target_pairs={{0,1},{1,2},{2,3},{3,4},{4,5},{5,6},{6,7},{7,0},{8,9},{9,10},{10,1... | collective-permute-start | bytes 1572872 | tf_op jit(solution)/shard_map/ppermute | solution.py:22
Sparse Core Ops, SparseCore 0:
  18.2 92.3 reduce-scatter.1
  114.8 50.9 all-reduce.1
